TPU v7x, 32 devices: a whole 2x2x4 slice. The times are simulated.
32 devices in a mesh: loop: 8 (over z, y), seg: 4 (over x, core).
Axes of the slice: x: 2, y: 2, z: 4, core: 2. Of those that a mesh axis runs over, the one named last changes fastest.
Arguments:
- dosage: bfloat16 [2048, 8192], P('seg', 'loop'), may hold values from -3 to 3
- weight_tiles: bfloat16 [3, 1024, 1024], P(None, None, 'loop'), may hold values from -0.109375 to 0.109375
- first_tile: int32 [1024], P('loop'), may hold values from 0 to 1
- last_tile: int32 [1024], P('loop'), may hold values from 1 to 2
Outputs:
- covariance: float32 [1024, 1024], P('seg', 'loop')
Inputs may be any that keep to these rules, and one draw needn't show every extreme that they name: `first_tile`: a gene's window always covers its home slot 1.
All inputs are finite; a program needn't handle non-finite values.
Results may differ from a plain program's by a relative error of at most 0.0021.
Values may be sent and summed in bfloat16 or wider, within the bound.
No kernel may reach another device: no remote copies, remote signals or barrier semaphores. Data moves between devices by JAX's collectives and lax.ppermute only.
A program may use at most 64 MiB of HBM per device.

v0:
```python
import functools
import math

import jax
import jax.numpy as jnp
import numpy as np
from jax import lax
from jax.experimental import pallas as pl
from jax.experimental.pallas import tpu as pltpu
from jax.sharding import PartitionSpec as P


AXES = ("loop", "seg")
DOSAGE_MAX, WEIGHT_MAX = 3.0, 0.109375
MASK_ROWS = 16


def ring_next(loop_size, place):
    if place % 2 == 0:
        return place + 2 if place + 2 < loop_size else loop_size - 1
    return place - 2 if place >= 3 else 0


def move(value, sizes, target):
    loop_size, seg_size = sizes
    pairs = []
    for place in range(loop_size):
        for part in range(seg_size):
            to = target(place, part)
            pairs.append((place * seg_size + part, to[0] * seg_size + to[1]))
    return lax.ppermute(value, AXES, pairs)


def stage_kernel(weights_ref, first_ref, last_ref, far_ref, near_ref, home_ref, tile_ref, window_ref, sems):
    place, part = lax.axis_index("loop"), lax.axis_index("seg")
    n_slots = weights_ref.shape[0]
    half = far_ref.shape[0]
    far_slot = (place % 2) * (n_slots - 1)
    near_slot = n_slots - 1 - far_slot
    rows = pl.ds(pl.multiple_of((part % 2) * half, half), half)
    copies = [
        pltpu.make_async_copy(weights_ref.at[far_slot, rows], far_ref, sems.at[0]),
        pltpu.make_async_copy(first_ref, window_ref.at[0], sems.at[1]),
        pltpu.make_async_copy(last_ref, window_ref.at[1], sems.at[2]),
        pltpu.make_async_copy(weights_ref.at[near_slot, rows], tile_ref, sems.at[3]),
        pltpu.make_async_copy(weights_ref.at[n_slots // 2], home_ref, sems.at[4]),
    ]
    for copy in copies:
        copy.start()
    for copy in copies[1:4]:
        copy.wait()
    first, last = window_ref[0], window_ref[1]
    covered = (near_slot >= first) & (near_slot <= last)
    near_ref[:half, :] = jnp.where(covered, tile_ref[...], jnp.zeros((), tile_ref.dtype))
    covered = (far_slot >= first) & (far_slot <= last) & (place > 0) & (place < lax.axis_size("loop") - 1)
    mask = jnp.where(covered, 1.0, 0.0)
    near_ref[half:, :] = jnp.broadcast_to(mask, (MASK_ROWS, mask.shape[1])).astype(near_ref.dtype)
    copies[0].wait()
    copies[4].wait()


def pair_kernel(n_blocks, where_ref, *refs):
    blocks, own_ref, away_refs = refs[:n_blocks], refs[n_blocks], refs[n_blocks + 1 : -2]
    column_ref, sums_ref = refs[-2:]
    genes = column_ref.shape[0]
    for k, block in enumerate(blocks):

        @pl.when(where_ref[2 * n_blocks] == k)
        def _():
            column_ref[...] = block[...]

    column = column_ref[...].T
    for k, block in enumerate(blocks):
        product = jnp.dot(block[...], column, preferred_element_type=jnp.float32)
        row = pl.multiple_of(where_ref[2 * k + 1] * genes, genes)
        sums_ref[where_ref[2 * k], pl.ds(row, genes), :] = product
    own_ref[...] = sums_ref[0]
    for j, away_ref in enumerate(away_refs):
        away_ref[...] = sums_ref[j + 1].astype(jnp.bfloat16)


def shards(dosage, weight_tiles, first_tile, last_tile):
    loop_size, seg_size = sizes = (lax.axis_size("loop"), lax.axis_size("seg"))
    place, part = lax.axis_index("loop"), lax.axis_index("seg")
    _, block, genes = weight_tiles.shape
    samples = dosage.shape[0]
    side = part % 2
    half = block // 2

    vmem = pl.BlockSpec(memory_space=pltpu.VMEM)
    hbm = pl.BlockSpec(memory_space=pltpu.HBM)
    tile_of = lambda n: jax.ShapeDtypeStruct((n, genes), weight_tiles.dtype)
    far_half, near_half, home_tile = pl.pallas_call(
        stage_kernel,
        out_shape=(tile_of(half), tile_of(half + MASK_ROWS), tile_of(block)),
        in_specs=[hbm] * 3,
        out_specs=[vmem] * 3,
        scratch_shapes=[pltpu.VMEM((half, genes), weight_tiles.dtype), pltpu.VMEM((2, 1, genes), jnp.int32), pltpu.SemaphoreType.DMA((5,))],
        compiler_params=pltpu.CompilerParams(vmem_limit_bytes=8 * block * genes * 2),
        name="stage",
    )(*[pltpu.with_memory_space_constraint(x, pltpu.HBM) for x in (weight_tiles, first_tile.reshape(1, -1), last_tile.reshape(1, -1))])

    def outward(step):
        def target(l, s):
            to = l + step if l % 2 else l - step
            return (to if 0 <= to < loop_size else (l if step == 1 else l ^ 1), s)

        return target

    partner = lambda l, s: (l ^ 1, s)
    sibling = lambda l, s: (l, s ^ 1)

    scale = 2.0 ** math.floor(math.log2(float(jnp.finfo(jnp.float16).max) / (block * DOSAGE_MAX * WEIGHT_MAX)))

    def packed(term):
        return (term * scale).astype(jnp.float16)

    def product(tile):
        return lax.dot_general(tile, dosage, (((0,), (1,)), ((), ())), preferred_element_type=jnp.float32)

    def term(mine, other):
        lower = jnp.where(side == 0, mine, other)
        upper = jnp.where(side == 0, other, mine)
        return product(jnp.concatenate([lower, upper], axis=0))

    far_half = move(far_half, sizes, outward(1))
    near_half = move(near_half, sizes, partner)
    home_term = product(home_tile)
    far_half, _ = lax.optimization_barrier((far_half, home_term))
    home_term = move(packed(home_term), sizes, partner)
    far_term = term(far_half, move(far_half, sizes, sibling))
    near_half, _ = lax.optimization_barrier((near_half, far_term))
    near_half, far_mask = near_half[:half], near_half[half]
    far_term = move(packed(far_term), sizes, outward(2))
    near_term = term(near_half, move(near_half, sizes, sibling))
    far_term = jnp.where(far_mask[:, None] > 0, far_term.astype(jnp.float32), 0.0)
    ready = lax.optimization_barrier(near_term + home_term.astype(jnp.float32) * (1.0 / scale))
    projection = (ready + far_term * (1.0 / scale)).astype(jnp.bfloat16)

    ahead = [ring_next(loop_size, l) for l in range(loop_size)]
    behind = [ahead.index(l) for l in range(loop_size)]
    blocks, sources = [projection], [list(range(loop_size))]
    forth = back = projection
    forth_from = back_from = sources[0]
    rounds = loop_size // 2 - 1
    for step in range(rounds):
        if step == rounds - 1:
            opposite = jnp.where(side == 0, forth, back)
            opposite = move(opposite, sizes, lambda l, s: (behind[behind[l]] if s % 2 else ahead[ahead[l]], s))
            opposite_from = [forth_from[behind[behind[l]]] for l in range(loop_size)]
        forth = move(forth, sizes, lambda l, s: (ahead[l], s))
        forth_from = [forth_from[behind[l]] for l in range(loop_size)]
        back = move(back, sizes, lambda l, s: (behind[l], s))
        back_from = [back_from[ahead[l]] for l in range(loop_size)]
        blocks += [forth, back]
        sources += [forth_from, back_from]
    blocks.append(opposite)
    sources.append(opposite_from)

    per_chunk = loop_size // seg_size
    held = np.array(sources).T ^ 1
    parts = np.arange(seg_size)[None, :, None]
    table = np.stack([(held[:, None, :] // per_chunk) ^ parts, np.broadcast_to((held % per_chunk)[:, None, :], (loop_size, seg_size, loop_size))], axis=-1)
    table = table.reshape(loop_size * seg_size, 2 * loop_size)
    own_genes = np.argmax(held == np.arange(loop_size)[:, None], axis=1)
    table = jnp.asarray(np.concatenate([table, np.repeat(own_genes, seg_size)[:, None]], axis=1), jnp.int32)
    where = lax.dynamic_slice(table, (place * seg_size + part, 0), (1, table.shape[1]))[0]
    rows = loop_size * genes // seg_size
    own, *away = pl.pallas_call(
        functools.partial(pair_kernel, loop_size),
        out_shape=[jax.ShapeDtypeStruct((rows, genes), jnp.float32)] + [jax.ShapeDtypeStruct((rows, genes), jnp.bfloat16)] * (seg_size - 1),
        in_specs=[pl.BlockSpec(memory_space=pltpu.SMEM)] + [vmem] * loop_size,
        out_specs=[vmem] * seg_size,
        scratch_shapes=[pltpu.VMEM((genes, samples), jnp.bfloat16), pltpu.VMEM((seg_size, rows, genes), jnp.float32)],
        compiler_params=pltpu.CompilerParams(vmem_limit_bytes=2 * (loop_size + 1) * genes * samples * 2 + 3 * seg_size * rows * genes * 4),
        name="pair_sums",
    )(where, *blocks)
    total = own
    for j in range(1, seg_size):
        total = total + move(away[j - 1], sizes, lambda l, s: (l, s ^ j)).astype(jnp.float32)
    return total / (samples * seg_size)


def solution(mesh):
    return jax.shard_map(
        shards,
        mesh=mesh,
        in_specs=(P("seg", "loop"), P(None, None, "loop"), P("loop"), P("loop")),
        out_specs=P("seg", "loop"),
        check_vma=False,
    )
```

profile of v0, /device:TPU:0, one launch (start us, length us, event | category | flops | bytes accessed | tf_op | source)
XLA Modules:
  0.0 49.7 jit_solution(16705756833166052297)
XLA Ops:
  0.0 0.0 copy-start
  0.0 1.2 %stage.1 = (bf16[512,128]{1,0:T(8,128)(2,1)S(1)}, bf16[528,128]{1,0:T(8,128)(2,1)S(1)}, bf16[1024,128]{1,0:T(8,128)(2,1)S(1)}) custom-call(bf16[3,1024,128]{2,1,0:T(8,128)(2,1)} %weights_ref.1, s32[1,128]{1,0:T(1,128)} %bitcast.10, s32[1,128]{1,0:T(1,128)} %bitcast.11), custom_call_target="tpu_custom_call" | custom-call | tf_op jit(solution)/shard_map/stage/pallas_call | solution.py:93
  1.2 0.7 %collective-permute-start.1 = (bf16[512,128]{1,0:T(8,128)(2,1)S(1)}, bf16[512,128]{1,0:T(8,128)(2,1)S(1)}, u32[]{:S(2)}, u32[]{:S(2)}) collective-permute-start(bf16[512,128]{1,0:T(8,128)(2,1)S(1)} %get-tuple-element.15), channel_id=1, source_target_pairs={{0,0},{1,1},{2,2},{3,3},{4,8},{5,9},{6,10},{7,11},{8,4},{9,5},{10,... | collective-permute-start | bytes 393224 | tf_op jit(solution)/shard_map/ppermute | solution.py:31
  1.9 0.0 copy-done
  1.9 0.5 multiply_convert_fusion.1
  2.4 0.0 collective-permute-done.1
  2.4 0.6 %collective-permute-start.2 = (bf16[512,128]{1,0:T(8,128)(2,1)S(1)}, bf16[512,128]{1,0:T(8,128)(2,1)S(1)}, u32[]{:S(2)}, u32[]{:S(2)}) collective-permute-start(bf16[512,128]{1,0:T(8,128)(2,1)S(1)} %collective-permute-done.1), channel_id=1, source_target_pairs={{0,1},{1,0},{2,3},{3,2},{4,5},{5,4},{6,7},{7,6},{8,9},{9,8},{10,11... | collective-permute-start | bytes 393224 | tf_op jit(solution)/shard_map/ppermute | solution.py:31
  3.0 9.3 %collective-permute-start = (bf16[528,128]{1,0:T(8,128)(2,1)S(1)}, bf16[528,128]{1,0:T(8,128)(2,1)S(1)}, u32[]{:S(2)}, u32[]{:S(2)}) collective-permute-start(bf16[528,128]{1,0:T(8,128)(2,1)S(1)} %get-tuple-element.14), channel_id=1, source_target_pairs={{0,4},{1,5},{2,6},{3,7},{4,0},{5,1},{6,2},{7,3},{8,12},{9,13},{10,... | collective-permute-start | bytes 405512 | tf_op jit(solution)/shard_map/ppermute | solution.py:31
  12.3 0.0 collective-permute-start.4
  12.3 0.0 collective-permute-done.2
  12.3 0.5 multiply_convert_fusion
  12.8 3.9 %collective-permute-done = bf16[528,128]{1,0:T(8,128)(2,1)S(1)} collective-permute-done((bf16[528,128]{1,0:T(8,128)(2,1)S(1)}, bf16[528,128]{1,0:T(8,128)(2,1)S(1)}, u32[]{:S(2)}, u32[]{:S(2)}) %collective-permute-start) | collective-permute-done | bytes 135200 | tf_op jit(solution)/shard_map/ppermute | solution.py:31
  16.7 0.1 collective-permute-start.3
  16.8 2.1 %collective-permute-start.5 = (f16[128,512]{1,0:T(8,128)(2,1)S(1)}, f16[128,512]{1,0:T(8,128)(2,1)S(1)}, u32[]{:S(2)}, u32[]{:S(2)}) collective-permute-start(f16[128,512]{1,0:T(8,128)(2,1)S(1)} %multiply_convert_fusion), channel_id=1, source_target_pairs={{0,4},{1,5},{2,6},{3,7},{4,12},{5,13},{6,14},{7,15},{8,0},{9,1},{1... | collective-permute-start | bytes 393224 | tf_op jit(solution)/shard_map/ppermute | solution.py:31
  18.9 0.0 collective-permute-done.3
  18.9 0.4 collective-permute-done.4
  19.3 0.5 convolution_add_fusion
  19.8 3.2 %collective-permute-done.5 = f16[128,512]{1,0:T(8,128)(2,1)S(1)} collective-permute-done((f16[128,512]{1,0:T(8,128)(2,1)S(1)}, f16[128,512]{1,0:T(8,128)(2,1)S(1)}, u32[]{:S(2)}, u32[]{:S(2)}) %collective-permute-start.5) | collective-permute-done | bytes 131104 | tf_op jit(solution)/shard_map/ppermute | solution.py:31
  23.0 0.1 add_convert_fusion.refs_0_
  23.1 1.7 %collective-permute-start.7 = (bf16[128,512]{1,0:T(8,128)(2,1)S(1)}, bf16[128,512]{1,0:T(8,128)(2,1)S(1)}, u32[]{:S(2)}, u32[]{:S(2)}) collective-permute-start(bf16[128,512]{1,0:T(8,128)(2,1)S(1)} %add_convert_fusion.refs_0_), channel_id=1, source_target_pairs={{0,4},{1,5},{2,6},{3,7},{4,12},{5,13},{6,14},{7,15},{8,0},{9,1},{1... | collective-permute-start | bytes 393224 | tf_op jit(solution)/shard_map/ppermute | solution.py:31
  24.9 0.3 collective-permute-start.6
  25.2 3.2 %collective-permute-done.7.refs_2_ = bf16[128,512]{1,0:T(8,128)(2,1)S(1)} collective-permute-done((bf16[128,512]{1,0:T(8,128)(2,1)S(1)}, bf16[128,512]{1,0:T(8,128)(2,1)S(1)}, u32[]{:S(2)}, u32[]{:S(2)}) %collective-permute-start.7) | collective-permute-done | bytes 131104 | tf_op jit(solution)/shard_map/ppermute | solution.py:31
  28.5 1.4 %collective-permute-start.9 = (bf16[128,512]{1,0:T(8,128)(2,1)S(1)}, bf16[128,512]{1,0:T(8,128)(2,1)S(1)}, u32[]{:S(2)}, u32[]{:S(2)}) collective-permute-start(bf16[128,512]{1,0:T(8,128)(2,1)S(1)} %collective-permute-done.7.refs_2_), channel_id=1, source_target_pairs={{0,4},{1,5},{2,6},{3,7},{4,12},{5,13},{6,14},{7,15},{8,0},{9,1},{1... | collective-permute-start | bytes 393224 | tf_op jit(solution)/shard_map/ppermute | solution.py:31
  29.9 0.0 collective-permute-done.6.refs_1_
  29.9 0.6 %collective-permute-start.8 = (bf16[128,512]{1,0:T(8,128)(2,1)S(1)}, bf16[128,512]{1,0:T(8,128)(2,1)S(1)}, u32[]{:S(2)}, u32[]{:S(2)}) collective-permute-start(bf16[128,512]{1,0:T(8,128)(2,1)S(1)} %collective-permute-done.6.refs_1_), channel_id=1, source_target_pairs={{0,8},{1,9},{2,10},{3,11},{4,0},{5,1},{6,2},{7,3},{8,16},{9,17},{1... | collective-permute-start | bytes 393224 | tf_op jit(solution)/shard_map/ppermute | solution.py:31
  30.5 2.9 %collective-permute-done.9.refs_4_ = bf16[128,512]{1,0:T(8,128)(2,1)S(1)} collective-permute-done((bf16[128,512]{1,0:T(8,128)(2,1)S(1)}, bf16[128,512]{1,0:T(8,128)(2,1)S(1)}, u32[]{:S(2)}, u32[]{:S(2)}) %collective-permute-start.9) | collective-permute-done | bytes 131104 | tf_op jit(solution)/shard_map/ppermute | solution.py:31
  33.4 1.4 %collective-permute-start.11 = (bf16[128,512]{1,0:T(8,128)(2,1)S(1)}, bf16[128,512]{1,0:T(8,128)(2,1)S(1)}, u32[]{:S(2)}, u32[]{:S(2)}) collective-permute-start(bf16[128,512]{1,0:T(8,128)(2,1)S(1)} %collective-permute-done.9.refs_4_), channel_id=1, source_target_pairs={{0,4},{1,5},{2,6},{3,7},{4,12},{5,13},{6,14},{7,15},{8,0},{9,1},{1... | collective-permute-start | bytes 393224 | tf_op jit(solution)/shard_map/ppermute | solution.py:31
  34.8 0.0 collective-permute-done.8.refs_3_
  34.9 1.6 %collective-permute-start.12 = (bf16[128,512]{1,0:T(8,128)(2,1)S(1)}, bf16[128,512]{1,0:T(8,128)(2,1)S(1)}, u32[]{:S(2)}, u32[]{:S(2)}) collective-permute-start(bf16[128,512]{1,0:T(8,128)(2,1)S(1)} %broadcast_select_fusion), channel_id=1, source_target_pairs={{0,16},{1,13},{2,18},{3,15},{4,8},{5,21},{6,10},{7,23},{8,24},{9,5... | collective-permute-start | bytes 393224 | tf_op jit(solution)/shard_map/ppermute | solution.py:31
  36.4 1.6 %collective-permute-start.10 = (bf16[128,512]{1,0:T(8,128)(2,1)S(1)}, bf16[128,512]{1,0:T(8,128)(2,1)S(1)}, u32[]{:S(2)}, u32[]{:S(2)}) collective-permute-start(bf16[128,512]{1,0:T(8,128)(2,1)S(1)} %collective-permute-done.8.refs_3_), channel_id=1, source_target_pairs={{0,8},{1,9},{2,10},{3,11},{4,0},{5,1},{6,2},{7,3},{8,16},{9,17},{1... | collective-permute-start | bytes 393224 | tf_op jit(solution)/shard_map/ppermute | solution.py:31
  38.0 0.7 %dynamic-slice_bitcast_fusion.where_ref = s32[17]{0:T(128)S(1)} fusion(s32[32,17]{1,0:T(8,128)} %constant.40.clone, s32[]{:T(128)S(6)} %select_n.42), kind=kLoop, calls=%fused_computation.18 | loop fusion | bytes 140 | tf_op jit(solution)/shard_map/squeeze | solution.py:167
  38.7 1.5 %collective-permute-done.11.refs_6_ = bf16[128,512]{1,0:T(8,128)(2,1)S(1)} collective-permute-done((bf16[128,512]{1,0:T(8,128)(2,1)S(1)}, bf16[128,512]{1,0:T(8,128)(2,1)S(1)}, u32[]{:S(2)}, u32[]{:S(2)}) %collective-permute-start.11) | collective-permute-done | bytes 131104 | tf_op jit(solution)/shard_map/ppermute | solution.py:31
  40.2 1.7 %collective-permute-done.12.refs_7_ = bf16[128,512]{1,0:T(8,128)(2,1)S(1)} collective-permute-done((bf16[128,512]{1,0:T(8,128)(2,1)S(1)}, bf16[128,512]{1,0:T(8,128)(2,1)S(1)}, u32[]{:S(2)}, u32[]{:S(2)}) %collective-permute-start.12) | collective-permute-done | bytes 131104 | tf_op jit(solution)/shard_map/ppermute | solution.py:31
  42.0 0.2 collective-permute-done.10.refs_5_
  42.2 1.1 %pair_sums.1 = (f32[256,128]{1,0:T(8,128)S(1)}, bf16[256,128]{1,0:T(8,128)(2,1)S(1)}, bf16[256,128]{1,0:T(8,128)(2,1)S(1)}, bf16[256,128]{1,0:T(8,128)(2,1)S(1)}) custom-call(s32[17]{0:T(128)S(1)} %dynamic-slice_bitcast_fusion.where_ref, bf16[128,512]{1,0:T(8,128)(2,1)S(1)} %add_convert_fusion.refs_0_, bf16[128,512]{1,0:T(8,128)(2,1)S(1)} %collective-permute-done.6.refs_1_, ...), custom_call_target="tpu_custom_call" | custom-call | tf_op jit(solution)/shard_map/pair_sums/pallas_call | solution.py:169
  43.3 0.1 collective-permute-start.13
  43.4 1.6 %collective-permute-start.14 = (bf16[256,128]{1,0:T(8,128)(2,1)S(1)}, bf16[256,128]{1,0:T(8,128)(2,1)S(1)}, u32[]{:S(2)}, u32[]{:S(2)}) collective-permute-start(bf16[256,128]{1,0:T(8,128)(2,1)S(1)} %get-tuple-element.21), channel_id=1, source_target_pairs={{0,2},{1,3},{2,0},{3,1},{4,6},{5,7},{6,4},{7,5},{8,10},{9,11},{10,... | collective-permute-start | bytes 196616 | tf_op jit(solution)/shard_map/ppermute | solution.py:31
  44.9 0.3 collective-permute-start.15
  45.2 0.0 collective-permute-done.13
  45.2 2.6 %collective-permute-done.14 = bf16[256,128]{1,0:T(8,128)(2,1)S(1)} collective-permute-done((bf16[256,128]{1,0:T(8,128)(2,1)S(1)}, bf16[256,128]{1,0:T(8,128)(2,1)S(1)}, u32[]{:S(2)}, u32[]{:S(2)}) %collective-permute-start.14) | collective-permute-done | bytes 65568 | tf_op jit(solution)/shard_map/ppermute | solution.py:31
  47.9 1.1 %collective-permute-done.15 = bf16[256,128]{1,0:T(8,128)(2,1)S(1)} collective-permute-done((bf16[256,128]{1,0:T(8,128)(2,1)S(1)}, bf16[256,128]{1,0:T(8,128)(2,1)S(1)}, u32[]{:S(2)}, u32[]{:S(2)}) %collective-permute-start.15) | collective-permute-done | bytes 65568 | tf_op jit(solution)/shard_map/ppermute | solution.py:31
  49.0 0.7 %add_multiply_fusion = f32[256,128]{1,0:T(8,128)} fusion(bf16[256,128]{1,0:T(8,128)(2,1)S(1)} %collective-permute-done.15, bf16[256,128]{1,0:T(8,128)(2,1)S(1)} %collective-permute-done.14, f32[256,128]{1,0:T(8,128)S(1)} %get-tuple-element.19, bf16[256,128]{1,0:T(8,128)(2,1)S(1)} %collective-permute-done.13), kind=kLoop, calls=%fused_computation.11 | loop fusion | flops 229376 | bytes 458752 | tf_op jit(solution)/shard_map/div | solution.py:181
  (5 shorter events, 0.1 us)
Async XLA Ops:
  0.0 1.9 %copy-start = (bf16[512,1024]{1,0:T(8,128)(2,1)S(1)}, bf16[512,1024]{1,0:T(8,128)(2,1)}, u32[]{:S(2)}) copy-start(bf16[512,1024]{1,0:T(8,128)(2,1)} %param.5) | copy-start | bytes 3145732
  1.2 1.2 %collective-permute-start.1 = (bf16[512,128]{1,0:T(8,128)(2,1)S(1)}, bf16[512,128]{1,0:T(8,128)(2,1)S(1)}, u32[]{:S(2)}, u32[]{:S(2)}) collective-permute-start(bf16[512,128]{1,0:T(8,128)(2,1)S(1)} %get-tuple-element.15), channel_id=1, source_target_pairs={{0,0},{1,1},{2,2},{3,3},{4,8},{5,9},{6,10},{7,11},{8,4},{9,5},{10,... | collective-permute-start | bytes 393224 | tf_op jit(solution)/shard_map/ppermute | solution.py:31
  2.4 9.9 %collective-permute-start.2 = (bf16[512,128]{1,0:T(8,128)(2,1)S(1)}, bf16[512,128]{1,0:T(8,128)(2,1)S(1)}, u32[]{:S(2)}, u32[]{:S(2)}) collective-permute-start(bf16[512,128]{1,0:T(8,128)(2,1)S(1)} %collective-permute-done.1), channel_id=1, source_target_pairs={{0,1},{1,0},{2,3},{3,2},{4,5},{5,4},{6,7},{7,6},{8,9},{9,8},{10,11... | collective-permute-start | bytes 393224 | tf_op jit(solution)/shard_map/ppermute | solution.py:31
  3.0 13.7 %collective-permute-start = (bf16[528,128]{1,0:T(8,128)(2,1)S(1)}, bf16[528,128]{1,0:T(8,128)(2,1)S(1)}, u32[]{:S(2)}, u32[]{:S(2)}) collective-permute-start(bf16[528,128]{1,0:T(8,128)(2,1)S(1)} %get-tuple-element.14), channel_id=1, source_target_pairs={{0,4},{1,5},{2,6},{3,7},{4,0},{5,1},{6,2},{7,3},{8,12},{9,13},{10,... | collective-permute-start | bytes 405512 | tf_op jit(solution)/shard_map/ppermute | solution.py:31
  12.3 7.1 %collective-permute-start.4 = (f16[128,512]{1,0:T(8,128)(2,1)S(1)}, f16[128,512]{1,0:T(8,128)(2,1)S(1)}, u32[]{:S(2)}, u32[]{:S(2)}) collective-permute-start(f16[128,512]{1,0:T(8,128)(2,1)S(1)} %multiply_convert_fusion.1), channel_id=1, source_target_pairs={{0,4},{1,5},{2,6},{3,7},{4,0},{5,1},{6,2},{7,3},{8,12},{9,13},{10,... | collective-permute-start | bytes 393224 | tf_op jit(solution)/shard_map/ppermute | solution.py:31
  16.7 2.2 %collective-permute-start.3 = (bf16[512,128]{1,0:T(8,128)(2,1)S(1)}, bf16[512,128]{1,0:T(8,128)(2,1)S(1)}, u32[]{:S(2)}, u32[]{:S(2)}) collective-permute-start(bf16[512,128]{1,0:T(8,128)(2,1)S(1)} %slice.6), channel_id=1, source_target_pairs={{0,1},{1,0},{2,3},{3,2},{4,5},{5,4},{6,7},{7,6},{8,9},{9,8},{10,11... | collective-permute-start | bytes 393224 | tf_op jit(solution)/shard_map/ppermute | solution.py:31
  16.8 6.2 %collective-permute-start.5 = (f16[128,512]{1,0:T(8,128)(2,1)S(1)}, f16[128,512]{1,0:T(8,128)(2,1)S(1)}, u32[]{:S(2)}, u32[]{:S(2)}) collective-permute-start(f16[128,512]{1,0:T(8,128)(2,1)S(1)} %multiply_convert_fusion), channel_id=1, source_target_pairs={{0,4},{1,5},{2,6},{3,7},{4,12},{5,13},{6,14},{7,15},{8,0},{9,1},{1... | collective-permute-start | bytes 393224 | tf_op jit(solution)/shard_map/ppermute | solution.py:31
  23.1 5.3 %collective-permute-start.7 = (bf16[128,512]{1,0:T(8,128)(2,1)S(1)}, bf16[128,512]{1,0:T(8,128)(2,1)S(1)}, u32[]{:S(2)}, u32[]{:S(2)}) collective-permute-start(bf16[128,512]{1,0:T(8,128)(2,1)S(1)} %add_convert_fusion.refs_0_), channel_id=1, source_target_pairs={{0,4},{1,5},{2,6},{3,7},{4,12},{5,13},{6,14},{7,15},{8,0},{9,1},{1... | collective-permute-start | bytes 393224 | tf_op jit(solution)/shard_map/ppermute | solution.py:31
  24.9 5.0 %collective-permute-start.6 = (bf16[128,512]{1,0:T(8,128)(2,1)S(1)}, bf16[128,512]{1,0:T(8,128)(2,1)S(1)}, u32[]{:S(2)}, u32[]{:S(2)}) collective-permute-start(bf16[128,512]{1,0:T(8,128)(2,1)S(1)} %add_convert_fusion.refs_0_), channel_id=1, source_target_pairs={{0,8},{1,9},{2,10},{3,11},{4,0},{5,1},{6,2},{7,3},{8,16},{9,17},{1... | collective-permute-start | bytes 393224 | tf_op jit(solution)/shard_map/ppermute | solution.py:31
  28.5 5.0 %collective-permute-start.9 = (bf16[128,512]{1,0:T(8,128)(2,1)S(1)}, bf16[128,512]{1,0:T(8,128)(2,1)S(1)}, u32[]{:S(2)}, u32[]{:S(2)}) collective-permute-start(bf16[128,512]{1,0:T(8,128)(2,1)S(1)} %collective-permute-done.7.refs_2_), channel_id=1, source_target_pairs={{0,4},{1,5},{2,6},{3,7},{4,12},{5,13},{6,14},{7,15},{8,0},{9,1},{1... | collective-permute-start | bytes 393224 | tf_op jit(solution)/shard_map/ppermute | solution.py:31
  29.9 5.0 %collective-permute-start.8 = (bf16[128,512]{1,0:T(8,128)(2,1)S(1)}, bf16[128,512]{1,0:T(8,128)(2,1)S(1)}, u32[]{:S(2)}, u32[]{:S(2)}) collective-permute-start(bf16[128,512]{1,0:T(8,128)(2,1)S(1)} %collective-permute-done.6.refs_1_), channel_id=1, source_target_pairs={{0,8},{1,9},{2,10},{3,11},{4,0},{5,1},{6,2},{7,3},{8,16},{9,17},{1... | collective-permute-start | bytes 393224 | tf_op jit(solution)/shard_map/ppermute | solution.py:31
  33.4 6.8 %collective-permute-start.11 = (bf16[128,512]{1,0:T(8,128)(2,1)S(1)}, bf16[128,512]{1,0:T(8,128)(2,1)S(1)}, u32[]{:S(2)}, u32[]{:S(2)}) collective-permute-start(bf16[128,512]{1,0:T(8,128)(2,1)S(1)} %collective-permute-done.9.refs_4_), channel_id=1, source_target_pairs={{0,4},{1,5},{2,6},{3,7},{4,12},{5,13},{6,14},{7,15},{8,0},{9,1},{1... | collective-permute-start | bytes 393224 | tf_op jit(solution)/shard_map/ppermute | solution.py:31
  34.9 7.1 %collective-permute-start.12 = (bf16[128,512]{1,0:T(8,128)(2,1)S(1)}, bf16[128,512]{1,0:T(8,128)(2,1)S(1)}, u32[]{:S(2)}, u32[]{:S(2)}) collective-permute-start(bf16[128,512]{1,0:T(8,128)(2,1)S(1)} %broadcast_select_fusion), channel_id=1, source_target_pairs={{0,16},{1,13},{2,18},{3,15},{4,8},{5,21},{6,10},{7,23},{8,24},{9,5... | collective-permute-start | bytes 393224 | tf_op jit(solution)/shard_map/ppermute | solution.py:31
  36.4 5.8 %collective-permute-start.10 = (bf16[128,512]{1,0:T(8,128)(2,1)S(1)}, bf16[128,512]{1,0:T(8,128)(2,1)S(1)}, u32[]{:S(2)}, u32[]{:S(2)}) collective-permute-start(bf16[128,512]{1,0:T(8,128)(2,1)S(1)} %collective-permute-done.8.refs_3_), channel_id=1, source_target_pairs={{0,8},{1,9},{2,10},{3,11},{4,0},{5,1},{6,2},{7,3},{8,16},{9,17},{1... | collective-permute-start | bytes 393224 | tf_op jit(solution)/shard_map/ppermute | solution.py:31
  43.3 1.9 %collective-permute-start.13 = (bf16[256,128]{1,0:T(8,128)(2,1)S(1)}, bf16[256,128]{1,0:T(8,128)(2,1)S(1)}, u32[]{:S(2)}, u32[]{:S(2)}) collective-permute-start(bf16[256,128]{1,0:T(8,128)(2,1)S(1)} %get-tuple-element.20), channel_id=1, source_target_pairs={{0,1},{1,0},{2,3},{3,2},{4,5},{5,4},{6,7},{7,6},{8,9},{9,8},{10,11... | collective-permute-start | bytes 196616 | tf_op jit(solution)/shard_map/ppermute | solution.py:31
  43.4 4.5 %collective-permute-start.14 = (bf16[256,128]{1,0:T(8,128)(2,1)S(1)}, bf16[256,128]{1,0:T(8,128)(2,1)S(1)}, u32[]{:S(2)}, u32[]{:S(2)}) collective-permute-start(bf16[256,128]{1,0:T(8,128)(2,1)S(1)} %get-tuple-element.21), channel_id=1, source_target_pairs={{0,2},{1,3},{2,0},{3,1},{4,6},{5,7},{6,4},{7,5},{8,10},{9,11},{10,... | collective-permute-start | bytes 196616 | tf_op jit(solution)/shard_map/ppermute | solution.py:31
  44.9 4.1 %collective-permute-start.15 = (bf16[256,128]{1,0:T(8,128)(2,1)S(1)}, bf16[256,128]{1,0:T(8,128)(2,1)S(1)}, u32[]{:S(2)}, u32[]{:S(2)}) collective-permute-start(bf16[256,128]{1,0:T(8,128)(2,1)S(1)} %get-tuple-element.22), channel_id=1, source_target_pairs={{0,3},{1,2},{2,1},{3,0},{4,7},{5,6},{6,5},{7,4},{8,11},{9,10},{10,... | collective-permute-start | bytes 196616 | tf_op jit(solution)/shard_map/ppermute | solution.py:31
where the time goes:
time: 49.8 us; the launch traced here: 49.7 us
  starting transfers between devices  23.3 us (47%)
  waiting for transfers between devices  20.9 us (42%)
  Pallas kernels  2.31 us (5%)
  matrix products  1.46 us (3%)
  other arithmetic  0.86 us (2%)
  local copies, waits for them, and re-layouts  0.7 us (1%)
    ppermute x16, starting transfers between devices, move(): return lax.ppermute(value, AXES, pairs)  23.3 us
    ppermute x16, waiting for transfers between devices, move(): return lax.ppermute(value, AXES, pairs)  20.9 us
    dot_general x3, matrix products, product(): lax.dot_general(tile, dosage, (((0,), (1,)), ((), ())), preferred_element...  1.46 us
    pallas_call x1, Pallas kernels, shards(): pl.pallas_call(stage_kernel, out_shape=(tile_of(half), tile_of(half + MAS...  1.24 us
    pallas_call x1, Pallas kernels, shards(): pl.pallas_call(functools.partial(pair_kernel, loop_size), out_shape=[jax....  1.07 us
  transfers between devices with their start and end apart: 16, of which 10 were waited for; matrix products, arithmetic and copies ran while one was open for 4% of the time, Pallas kernels for 0%

commit v1 on v0

--- a/solution.py
+++ b/solution.py
@@ -31,23 +31,22 @@
     return lax.ppermute(value, AXES, pairs)
 
 
-def stage_kernel(weights_ref, first_ref, last_ref, far_ref, near_ref, home_ref, tile_ref, window_ref, sems):
+def stage_kernel(weights_ref, first_ref, last_ref, near_ref, home_ref, tile_ref, window_ref, sems):
     place, part = lax.axis_index("loop"), lax.axis_index("seg")
     n_slots = weights_ref.shape[0]
-    half = far_ref.shape[0]
+    half = tile_ref.shape[0]
     far_slot = (place % 2) * (n_slots - 1)
     near_slot = n_slots - 1 - far_slot
     rows = pl.ds(pl.multiple_of((part % 2) * half, half), half)
     copies = [
-        pltpu.make_async_copy(weights_ref.at[far_slot, rows], far_ref, sems.at[0]),
-        pltpu.make_async_copy(first_ref, window_ref.at[0], sems.at[1]),
-        pltpu.make_async_copy(last_ref, window_ref.at[1], sems.at[2]),
-        pltpu.make_async_copy(weights_ref.at[near_slot, rows], tile_ref, sems.at[3]),
-        pltpu.make_async_copy(weights_ref.at[n_slots // 2], home_ref, sems.at[4]),
+        pltpu.make_async_copy(first_ref, window_ref.at[0], sems.at[0]),
+        pltpu.make_async_copy(last_ref, window_ref.at[1], sems.at[1]),
+        pltpu.make_async_copy(weights_ref.at[near_slot, rows], tile_ref, sems.at[2]),
+        pltpu.make_async_copy(weights_ref.at[n_slots // 2], home_ref, sems.at[3]),
     ]
     for copy in copies:
         copy.start()
-    for copy in copies[1:4]:
+    for copy in copies[:3]:
         copy.wait()
     first, last = window_ref[0], window_ref[1]
     covered = (near_slot >= first) & (near_slot <= last)
@@ -55,8 +54,7 @@
     covered = (far_slot >= first) & (far_slot <= last) & (place > 0) & (place < lax.axis_size("loop") - 1)
     mask = jnp.where(covered, 1.0, 0.0)
     near_ref[half:, :] = jnp.broadcast_to(mask, (MASK_ROWS, mask.shape[1])).astype(near_ref.dtype)
-    copies[0].wait()
-    copies[4].wait()
+    copies[3].wait()
 
 
 def pair_kernel(n_blocks, where_ref, *refs):
@@ -82,7 +80,7 @@
 def shards(dosage, weight_tiles, first_tile, last_tile):
     loop_size, seg_size = sizes = (lax.axis_size("loop"), lax.axis_size("seg"))
     place, part = lax.axis_index("loop"), lax.axis_index("seg")
-    _, block, genes = weight_tiles.shape
+    n_slots, block, genes = weight_tiles.shape
     samples = dosage.shape[0]
     side = part % 2
     half = block // 2
@@ -90,20 +88,24 @@
     vmem = pl.BlockSpec(memory_space=pltpu.VMEM)
     hbm = pl.BlockSpec(memory_space=pltpu.HBM)
     tile_of = lambda n: jax.ShapeDtypeStruct((n, genes), weight_tiles.dtype)
-    far_half, near_half, home_tile = pl.pallas_call(
+    far_half = lax.dynamic_slice(weight_tiles, ((place % 2) * (n_slots - 1), side * half, 0), (1, half, genes))[0]
+    near_half, home_tile = pl.pallas_call(
         stage_kernel,
-        out_shape=(tile_of(half), tile_of(half + MASK_ROWS), tile_of(block)),
+        out_shape=(tile_of(half + MASK_ROWS), tile_of(block)),
         in_specs=[hbm] * 3,
-        out_specs=[vmem] * 3,
-        scratch_shapes=[pltpu.VMEM((half, genes), weight_tiles.dtype), pltpu.VMEM((2, 1, genes), jnp.int32), pltpu.SemaphoreType.DMA((5,))],
+        out_specs=[vmem] * 2,
+        scratch_shapes=[pltpu.VMEM((half, genes), weight_tiles.dtype), pltpu.VMEM((2, 1, genes), jnp.int32), pltpu.SemaphoreType.DMA((4,))],
         compiler_params=pltpu.CompilerParams(vmem_limit_bytes=8 * block * genes * 2),
         name="stage",
+        cost_estimate=pl.CostEstimate(flops=0, bytes_accessed=4 * block * genes, transcendentals=0),
     )(*[pltpu.with_memory_space_constraint(x, pltpu.HBM) for x in (weight_tiles, first_tile.reshape(1, -1), last_tile.reshape(1, -1))])
 
     def outward(step):
         def target(l, s):
             to = l + step if l % 2 else l - step
-            return (to if 0 <= to < loop_size else (l if step == 1 else l ^ 1), s)
+            if 0 <= to < loop_size:
+                return to, s
+            return (l, s ^ 1) if step == 1 else (l ^ 1, s)
 
         return target
 

time: 49.8 us -> 47.8 us (0.960)
  starting transfers between devices: 23.3 us -> 20.3 us
  local copies, waits for them, and re-layouts: 0.7 us -> 1.71 us
    ppermute x16, starting transfers between devices: 23.3 us -> 20.3 us  [move(): return lax.ppermute(value, AXES, pairs)]
    squeeze x0 -> x1, local copies, waits for them, and re-layouts: none -> 1 us  [shards(): lax.dynamic_slice(weight_tiles, (place % 2 * (n_slots - 1), side * half,...]
  transfers between devices with their start and end apart: 16 -> 16, of which waited for: 10 -> 10; matrix products, arithmetic and copies ran while one was open for 4% -> 5% of each run, Pallas kernels for 0% -> 2%
where the time goes in v1:
time: 47.8 us; the launch traced here: 47.6 us
  waiting for transfers between devices  20.9 us (44%)
  starting transfers between devices  20.3 us (42%)
  Pallas kernels  2.15 us (4%)
  local copies, waits for them, and re-layouts  1.71 us (4%)
  matrix products  1.45 us (3%)
  other arithmetic  0.86 us (2%)
    ppermute x16, waiting for transfers between devices, move(): return lax.ppermute(value, AXES, pairs)  20.9 us
    ppermute x16, starting transfers between devices, move(): return lax.ppermute(value, AXES, pairs)  20.3 us
    dot_general x3, matrix products, product(): lax.dot_general(tile, dosage, (((0,), (1,)), ((), ())), preferred_element...  1.45 us
    pallas_call x1, Pallas kernels, shards(): pl.pallas_call(stage_kernel, out_shape=(tile_of(half + MASK_ROWS), tile_o...  1.08 us
    pallas_call x1, Pallas kernels, shards(): pl.pallas_call(functools.partial(pair_kernel, loop_size), out_shape=[jax....  1.07 us
    squeeze x1, local copies, waits for them, and re-layouts, shards(): lax.dynamic_slice(weight_tiles, (place % 2 * (n_slots - 1), side * half,...  1 us
  transfers between devices with their start and end apart: 16, of which 10 were waited for; matrix products, arithmetic and copies ran while one was open for 5% of the time, Pallas kernels for 2%

profile of v1, /device:TPU:0, one launch (start us, length us, event | category | flops | bytes accessed | tf_op | source)
XLA Modules:
  0.0 47.6 jit_solution(12073227113404554645)
XLA Ops:
  0.0 0.0 copy-start
  0.0 1.0 %dynamic-slice_bitcast_fusion = bf16[512,128]{1,0:T(8,128)(2,1)S(1)} fusion(bf16[3,1024,128]{2,1,0:T(8,128)(2,1)} %weights_ref.1, s32[]{:T(128)S(6)} %select_n.56, s32[]{:T(128)S(6)} %select_n.57), kind=kLoop, calls=%fused_computation.12 | loop fusion | bytes 262152 | tf_op jit(solution)/shard_map/squeeze | solution.py:91
  1.0 0.6 %collective-permute-start.1 = (bf16[512,128]{1,0:T(8,128)(2,1)S(1)}, bf16[512,128]{1,0:T(8,128)(2,1)S(1)}, u32[]{:S(2)}, u32[]{:S(2)}) collective-permute-start(bf16[512,128]{1,0:T(8,128)(2,1)S(1)} %dynamic-slice_bitcast_fusion), channel_id=1, source_target_pairs={{0,1},{1,0},{2,3},{3,2},{4,8},{5,9},{6,10},{7,11},{8,4},{9,5},{10,... | collective-permute-start | bytes 393224 | tf_op jit(solution)/shard_map/ppermute | solution.py:31
  1.6 1.1 %stage.1 = (bf16[528,128]{1,0:T(8,128)(2,1)S(1)}, bf16[1024,128]{1,0:T(8,128)(2,1)S(1)}) custom-call(bf16[3,1024,128]{2,1,0:T(8,128)(2,1)} %weights_ref.1, s32[1,128]{1,0:T(1,128)} %bitcast.12, s32[1,128]{1,0:T(1,128)} %bitcast.13), custom_call_target="tpu_custom_call" | custom-call | bytes 524288 | tf_op jit(solution)/shard_map/stage/pallas_call | solution.py:92
  2.7 0.0 copy-done
  2.7 0.5 %multiply_convert_fusion.1 = f16[128,512]{1,0:T(8,128)(2,1)S(1)} fusion(bf16[1024,128]{1,0:T(8,128)(2,1)S(1)} %get-tuple-element.14, bf16[512,1024]{1,0:T(8,128)(2,1)S(1)} %copy-done), kind=kOutput, calls=%fused_computation.10 | convolution fusion | flops 134348800 | bytes 1441792 | tf_op jit(solution)/shard_map/dot_general | solution.py:121
  3.2 0.0 collective-permute-done.1
  3.2 0.1 collective-permute-start.2
  3.3 7.0 %collective-permute-start = (bf16[528,128]{1,0:T(8,128)(2,1)S(1)}, bf16[528,128]{1,0:T(8,128)(2,1)S(1)}, u32[]{:S(2)}, u32[]{:S(2)}) collective-permute-start(bf16[528,128]{1,0:T(8,128)(2,1)S(1)} %get-tuple-element.13), channel_id=1, source_target_pairs={{0,4},{1,5},{2,6},{3,7},{4,0},{5,1},{6,2},{7,3},{8,12},{9,13},{10,... | collective-permute-start | bytes 405512 | tf_op jit(solution)/shard_map/ppermute | solution.py:31
  10.2 0.0 collective-permute-start.4
  10.2 0.0 collective-permute-done.2
  10.3 0.5 %multiply_convert_fusion = f16[128,512]{1,0:T(8,128)(2,1)S(1)} fusion(bf16[512,1024]{1,0:T(8,128)(2,1)S(1)} %copy-done, bf16[512,128]{1,0:T(8,128)(2,1)S(1)} %get-tuple-element.24, bf16[512,128]{1,0:T(8,128)(2,1)S(1)} %get-tuple-element.23), kind=kOutput, calls=%fused_computation.9 | convolution fusion | flops 134873088 | bytes 1441792 | tf_op jit(solution)/shard_map/dot_general | solution.py:121
  10.8 3.9 %collective-permute-done = bf16[528,128]{1,0:T(8,128)(2,1)S(1)} collective-permute-done((bf16[528,128]{1,0:T(8,128)(2,1)S(1)}, bf16[528,128]{1,0:T(8,128)(2,1)S(1)}, u32[]{:S(2)}, u32[]{:S(2)}) %collective-permute-start) | collective-permute-done | bytes 135200 | tf_op jit(solution)/shard_map/ppermute | solution.py:31
  14.7 0.1 collective-permute-start.3
  14.7 2.1 %collective-permute-start.5 = (f16[128,512]{1,0:T(8,128)(2,1)S(1)}, f16[128,512]{1,0:T(8,128)(2,1)S(1)}, u32[]{:S(2)}, u32[]{:S(2)}) collective-permute-start(f16[128,512]{1,0:T(8,128)(2,1)S(1)} %multiply_convert_fusion), channel_id=1, source_target_pairs={{0,4},{1,5},{2,6},{3,7},{4,12},{5,13},{6,14},{7,15},{8,0},{9,1},{1... | collective-permute-start | bytes 393224 | tf_op jit(solution)/shard_map/ppermute | solution.py:31
  16.8 0.0 collective-permute-done.3
  16.9 0.4 collective-permute-done.4
  17.3 0.5 %convolution_add_fusion = f32[128,512]{1,0:T(8,128)S(1)} fusion(bf16[512,1024]{1,0:T(8,128)(2,1)S(1)} %copy-done, bf16[512,128]{1,0:T(8,128)(2,1)S(1)} %get-tuple-element.22, bf16[512,128]{1,0:T(8,128)(2,1)S(1)} %get-tuple-element.21, f16[128,512]{1,0:T(8,128)(2,1)S(1)} %collective-permute-done.4), kind=kOutput, calls=%fused_computation | convolution fusion | flops 134938624 | bytes 1703936 | tf_op jit(solution)/shard_map/dot_general | solution.py:121
  17.8 3.2 %collective-permute-done.5 = f16[128,512]{1,0:T(8,128)(2,1)S(1)} collective-permute-done((f16[128,512]{1,0:T(8,128)(2,1)S(1)}, f16[128,512]{1,0:T(8,128)(2,1)S(1)}, u32[]{:S(2)}, u32[]{:S(2)}) %collective-permute-start.5) | collective-permute-done | bytes 131104 | tf_op jit(solution)/shard_map/ppermute | solution.py:31
  21.0 0.1 add_convert_fusion.refs_0_
  21.1 1.7 %collective-permute-start.7 = (bf16[128,512]{1,0:T(8,128)(2,1)S(1)}, bf16[128,512]{1,0:T(8,128)(2,1)S(1)}, u32[]{:S(2)}, u32[]{:S(2)}) collective-permute-start(bf16[128,512]{1,0:T(8,128)(2,1)S(1)} %add_convert_fusion.refs_0_), channel_id=1, source_target_pairs={{0,4},{1,5},{2,6},{3,7},{4,12},{5,13},{6,14},{7,15},{8,0},{9,1},{1... | collective-permute-start | bytes 393224 | tf_op jit(solution)/shard_map/ppermute | solution.py:31
  22.8 0.3 collective-permute-start.6
  23.2 3.2 %collective-permute-done.7.refs_2_ = bf16[128,512]{1,0:T(8,128)(2,1)S(1)} collective-permute-done((bf16[128,512]{1,0:T(8,128)(2,1)S(1)}, bf16[128,512]{1,0:T(8,128)(2,1)S(1)}, u32[]{:S(2)}, u32[]{:S(2)}) %collective-permute-start.7) | collective-permute-done | bytes 131104 | tf_op jit(solution)/shard_map/ppermute | solution.py:31
  26.4 1.4 %collective-permute-start.9 = (bf16[128,512]{1,0:T(8,128)(2,1)S(1)}, bf16[128,512]{1,0:T(8,128)(2,1)S(1)}, u32[]{:S(2)}, u32[]{:S(2)}) collective-permute-start(bf16[128,512]{1,0:T(8,128)(2,1)S(1)} %collective-permute-done.7.refs_2_), channel_id=1, source_target_pairs={{0,4},{1,5},{2,6},{3,7},{4,12},{5,13},{6,14},{7,15},{8,0},{9,1},{1... | collective-permute-start | bytes 393224 | tf_op jit(solution)/shard_map/ppermute | solution.py:31
  27.8 0.0 collective-permute-done.6.refs_1_
  27.8 0.6 %collective-permute-start.8 = (bf16[128,512]{1,0:T(8,128)(2,1)S(1)}, bf16[128,512]{1,0:T(8,128)(2,1)S(1)}, u32[]{:S(2)}, u32[]{:S(2)}) collective-permute-start(bf16[128,512]{1,0:T(8,128)(2,1)S(1)} %collective-permute-done.6.refs_1_), channel_id=1, source_target_pairs={{0,8},{1,9},{2,10},{3,11},{4,0},{5,1},{6,2},{7,3},{8,16},{9,17},{1... | collective-permute-start | bytes 393224 | tf_op jit(solution)/shard_map/ppermute | solution.py:31
  28.4 2.9 %collective-permute-done.9.refs_4_ = bf16[128,512]{1,0:T(8,128)(2,1)S(1)} collective-permute-done((bf16[128,512]{1,0:T(8,128)(2,1)S(1)}, bf16[128,512]{1,0:T(8,128)(2,1)S(1)}, u32[]{:S(2)}, u32[]{:S(2)}) %collective-permute-start.9) | collective-permute-done | bytes 131104 | tf_op jit(solution)/shard_map/ppermute | solution.py:31
  31.4 1.4 %collective-permute-start.11 = (bf16[128,512]{1,0:T(8,128)(2,1)S(1)}, bf16[128,512]{1,0:T(8,128)(2,1)S(1)}, u32[]{:S(2)}, u32[]{:S(2)}) collective-permute-start(bf16[128,512]{1,0:T(8,128)(2,1)S(1)} %collective-permute-done.9.refs_4_), channel_id=1, source_target_pairs={{0,4},{1,5},{2,6},{3,7},{4,12},{5,13},{6,14},{7,15},{8,0},{9,1},{1... | collective-permute-start | bytes 393224 | tf_op jit(solution)/shard_map/ppermute | solution.py:31
  32.8 0.0 collective-permute-done.8.refs_3_
  32.8 1.6 %collective-permute-start.12 = (bf16[128,512]{1,0:T(8,128)(2,1)S(1)}, bf16[128,512]{1,0:T(8,128)(2,1)S(1)}, u32[]{:S(2)}, u32[]{:S(2)}) collective-permute-start(bf16[128,512]{1,0:T(8,128)(2,1)S(1)} %broadcast_select_fusion), channel_id=1, source_target_pairs={{0,16},{1,13},{2,18},{3,15},{4,8},{5,21},{6,10},{7,23},{8,24},{9,5... | collective-permute-start | bytes 393224 | tf_op jit(solution)/shard_map/ppermute | solution.py:31
  34.4 1.6 %collective-permute-start.10 = (bf16[128,512]{1,0:T(8,128)(2,1)S(1)}, bf16[128,512]{1,0:T(8,128)(2,1)S(1)}, u32[]{:S(2)}, u32[]{:S(2)}) collective-permute-start(bf16[128,512]{1,0:T(8,128)(2,1)S(1)} %collective-permute-done.8.refs_3_), channel_id=1, source_target_pairs={{0,8},{1,9},{2,10},{3,11},{4,0},{5,1},{6,2},{7,3},{8,16},{9,17},{1... | collective-permute-start | bytes 393224 | tf_op jit(solution)/shard_map/ppermute | solution.py:31
  36.0 0.7 %dynamic-slice_bitcast_fusion.1.where_ref = s32[17]{0:T(128)S(1)} fusion(s32[32,17]{1,0:T(8,128)} %constant.50.clone, s32[]{:T(128)S(6)} %select_n.52), kind=kLoop, calls=%fused_computation.19 | loop fusion | bytes 140 | tf_op jit(solution)/shard_map/squeeze | solution.py:169
  36.6 1.5 %collective-permute-done.11.refs_6_ = bf16[128,512]{1,0:T(8,128)(2,1)S(1)} collective-permute-done((bf16[128,512]{1,0:T(8,128)(2,1)S(1)}, bf16[128,512]{1,0:T(8,128)(2,1)S(1)}, u32[]{:S(2)}, u32[]{:S(2)}) %collective-permute-start.11) | collective-permute-done | bytes 131104 | tf_op jit(solution)/shard_map/ppermute | solution.py:31
  38.2 1.7 %collective-permute-done.12.refs_7_ = bf16[128,512]{1,0:T(8,128)(2,1)S(1)} collective-permute-done((bf16[128,512]{1,0:T(8,128)(2,1)S(1)}, bf16[128,512]{1,0:T(8,128)(2,1)S(1)}, u32[]{:S(2)}, u32[]{:S(2)}) %collective-permute-start.12) | collective-permute-done | bytes 131104 | tf_op jit(solution)/shard_map/ppermute | solution.py:31
  39.9 0.2 collective-permute-done.10.refs_5_
  40.1 1.1 %pair_sums.1 = (f32[256,128]{1,0:T(8,128)S(1)}, bf16[256,128]{1,0:T(8,128)(2,1)S(1)}, bf16[256,128]{1,0:T(8,128)(2,1)S(1)}, bf16[256,128]{1,0:T(8,128)(2,1)S(1)}) custom-call(s32[17]{0:T(128)S(1)} %dynamic-slice_bitcast_fusion.1.where_ref, bf16[128,512]{1,0:T(8,128)(2,1)S(1)} %add_convert_fusion.refs_0_, ...), custom_call_target="tpu_custom_call" | custom-call | tf_op jit(solution)/shard_map/pair_sums/pallas_call | solution.py:171
  41.2 0.1 collective-permute-start.13
  41.3 1.6 %collective-permute-start.14 = (bf16[256,128]{1,0:T(8,128)(2,1)S(1)}, bf16[256,128]{1,0:T(8,128)(2,1)S(1)}, u32[]{:S(2)}, u32[]{:S(2)}) collective-permute-start(bf16[256,128]{1,0:T(8,128)(2,1)S(1)} %get-tuple-element.19), channel_id=1, source_target_pairs={{0,2},{1,3},{2,0},{3,1},{4,6},{5,7},{6,4},{7,5},{8,10},{9,11},{10,... | collective-permute-start | bytes 196616 | tf_op jit(solution)/shard_map/ppermute | solution.py:31
  42.8 0.3 collective-permute-start.15
  43.1 0.0 collective-permute-done.13
  43.1 2.6 %collective-permute-done.14 = bf16[256,128]{1,0:T(8,128)(2,1)S(1)} collective-permute-done((bf16[256,128]{1,0:T(8,128)(2,1)S(1)}, bf16[256,128]{1,0:T(8,128)(2,1)S(1)}, u32[]{:S(2)}, u32[]{:S(2)}) %collective-permute-start.14) | collective-permute-done | bytes 65568 | tf_op jit(solution)/shard_map/ppermute | solution.py:31
  45.8 1.1 %collective-permute-done.15 = bf16[256,128]{1,0:T(8,128)(2,1)S(1)} collective-permute-done((bf16[256,128]{1,0:T(8,128)(2,1)S(1)}, bf16[256,128]{1,0:T(8,128)(2,1)S(1)}, u32[]{:S(2)}, u32[]{:S(2)}) %collective-permute-start.15) | collective-permute-done | bytes 65568 | tf_op jit(solution)/shard_map/ppermute | solution.py:31
  46.9 0.7 %add_multiply_fusion = f32[256,128]{1,0:T(8,128)} fusion(bf16[256,128]{1,0:T(8,128)(2,1)S(1)} %collective-permute-done.15, bf16[256,128]{1,0:T(8,128)(2,1)S(1)} %collective-permute-done.14, f32[256,128]{1,0:T(8,128)S(1)} %get-tuple-element.17, bf16[256,128]{1,0:T(8,128)(2,1)S(1)} %collective-permute-done.13), kind=kLoop, calls=%fused_computation.11 | loop fusion | flops 229376 | bytes 458752 | tf_op jit(solution)/shard_map/div | solution.py:183
  (5 shorter events, 0.1 us)
Async XLA Ops:
  0.0 2.7 %copy-start = (bf16[512,1024]{1,0:T(8,128)(2,1)S(1)}, bf16[512,1024]{1,0:T(8,128)(2,1)}, u32[]{:S(2)}) copy-start(bf16[512,1024]{1,0:T(8,128)(2,1)} %param.5) | copy-start | bytes 3145732
  1.0 2.2 %collective-permute-start.1 = (bf16[512,128]{1,0:T(8,128)(2,1)S(1)}, bf16[512,128]{1,0:T(8,128)(2,1)S(1)}, u32[]{:S(2)}, u32[]{:S(2)}) collective-permute-start(bf16[512,128]{1,0:T(8,128)(2,1)S(1)} %dynamic-slice_bitcast_fusion), channel_id=1, source_target_pairs={{0,1},{1,0},{2,3},{3,2},{4,8},{5,9},{6,10},{7,11},{8,4},{9,5},{10,... | collective-permute-start | bytes 393224 | tf_op jit(solution)/shard_map/ppermute | solution.py:31
  3.2 7.1 %collective-permute-start.2 = (bf16[512,128]{1,0:T(8,128)(2,1)S(1)}, bf16[512,128]{1,0:T(8,128)(2,1)S(1)}, u32[]{:S(2)}, u32[]{:S(2)}) collective-permute-start(bf16[512,128]{1,0:T(8,128)(2,1)S(1)} %collective-permute-done.1), channel_id=1, source_target_pairs={{0,1},{1,0},{2,3},{3,2},{4,5},{5,4},{6,7},{7,6},{8,9},{9,8},{10,11... | collective-permute-start | bytes 393224 | tf_op jit(solution)/shard_map/ppermute | solution.py:31
  3.3 11.4 %collective-permute-start = (bf16[528,128]{1,0:T(8,128)(2,1)S(1)}, bf16[528,128]{1,0:T(8,128)(2,1)S(1)}, u32[]{:S(2)}, u32[]{:S(2)}) collective-permute-start(bf16[528,128]{1,0:T(8,128)(2,1)S(1)} %get-tuple-element.13), channel_id=1, source_target_pairs={{0,4},{1,5},{2,6},{3,7},{4,0},{5,1},{6,2},{7,3},{8,12},{9,13},{10,... | collective-permute-start | bytes 405512 | tf_op jit(solution)/shard_map/ppermute | solution.py:31
  10.2 7.1 %collective-permute-start.4 = (f16[128,512]{1,0:T(8,128)(2,1)S(1)}, f16[128,512]{1,0:T(8,128)(2,1)S(1)}, u32[]{:S(2)}, u32[]{:S(2)}) collective-permute-start(f16[128,512]{1,0:T(8,128)(2,1)S(1)} %multiply_convert_fusion.1), channel_id=1, source_target_pairs={{0,4},{1,5},{2,6},{3,7},{4,0},{5,1},{6,2},{7,3},{8,12},{9,13},{10,... | collective-permute-start | bytes 393224 | tf_op jit(solution)/shard_map/ppermute | solution.py:31
  14.7 2.2 %collective-permute-start.3 = (bf16[512,128]{1,0:T(8,128)(2,1)S(1)}, bf16[512,128]{1,0:T(8,128)(2,1)S(1)}, u32[]{:S(2)}, u32[]{:S(2)}) collective-permute-start(bf16[512,128]{1,0:T(8,128)(2,1)S(1)} %slice.6), channel_id=1, source_target_pairs={{0,1},{1,0},{2,3},{3,2},{4,5},{5,4},{6,7},{7,6},{8,9},{9,8},{10,11... | collective-permute-start | bytes 393224 | tf_op jit(solution)/shard_map/ppermute | solution.py:31
  14.7 6.2 %collective-permute-start.5 = (f16[128,512]{1,0:T(8,128)(2,1)S(1)}, f16[128,512]{1,0:T(8,128)(2,1)S(1)}, u32[]{:S(2)}, u32[]{:S(2)}) collective-permute-start(f16[128,512]{1,0:T(8,128)(2,1)S(1)} %multiply_convert_fusion), channel_id=1, source_target_pairs={{0,4},{1,5},{2,6},{3,7},{4,12},{5,13},{6,14},{7,15},{8,0},{9,1},{1... | collective-permute-start | bytes 393224 | tf_op jit(solution)/shard_map/ppermute | solution.py:31
  21.1 5.3 %collective-permute-start.7 = (bf16[128,512]{1,0:T(8,128)(2,1)S(1)}, bf16[128,512]{1,0:T(8,128)(2,1)S(1)}, u32[]{:S(2)}, u32[]{:S(2)}) collective-permute-start(bf16[128,512]{1,0:T(8,128)(2,1)S(1)} %add_convert_fusion.refs_0_), channel_id=1, source_target_pairs={{0,4},{1,5},{2,6},{3,7},{4,12},{5,13},{6,14},{7,15},{8,0},{9,1},{1... | collective-permute-start | bytes 393224 | tf_op jit(solution)/shard_map/ppermute | solution.py:31
  22.8 5.0 %collective-permute-start.6 = (bf16[128,512]{1,0:T(8,128)(2,1)S(1)}, bf16[128,512]{1,0:T(8,128)(2,1)S(1)}, u32[]{:S(2)}, u32[]{:S(2)}) collective-permute-start(bf16[128,512]{1,0:T(8,128)(2,1)S(1)} %add_convert_fusion.refs_0_), channel_id=1, source_target_pairs={{0,8},{1,9},{2,10},{3,11},{4,0},{5,1},{6,2},{7,3},{8,16},{9,17},{1... | collective-permute-start | bytes 393224 | tf_op jit(solution)/shard_map/ppermute | solution.py:31
  26.4 5.0 %collective-permute-start.9 = (bf16[128,512]{1,0:T(8,128)(2,1)S(1)}, bf16[128,512]{1,0:T(8,128)(2,1)S(1)}, u32[]{:S(2)}, u32[]{:S(2)}) collective-permute-start(bf16[128,512]{1,0:T(8,128)(2,1)S(1)} %collective-permute-done.7.refs_2_), channel_id=1, source_target_pairs={{0,4},{1,5},{2,6},{3,7},{4,12},{5,13},{6,14},{7,15},{8,0},{9,1},{1... | collective-permute-start | bytes 393224 | tf_op jit(solution)/shard_map/ppermute | solution.py:31
  27.8 5.0 %collective-permute-start.8 = (bf16[128,512]{1,0:T(8,128)(2,1)S(1)}, bf16[128,512]{1,0:T(8,128)(2,1)S(1)}, u32[]{:S(2)}, u32[]{:S(2)}) collective-permute-start(bf16[128,512]{1,0:T(8,128)(2,1)S(1)} %collective-permute-done.6.refs_1_), channel_id=1, source_target_pairs={{0,8},{1,9},{2,10},{3,11},{4,0},{5,1},{6,2},{7,3},{8,16},{9,17},{1... | collective-permute-start | bytes 393224 | tf_op jit(solution)/shard_map/ppermute | solution.py:31
  31.4 6.8 %collective-permute-start.11 = (bf16[128,512]{1,0:T(8,128)(2,1)S(1)}, bf16[128,512]{1,0:T(8,128)(2,1)S(1)}, u32[]{:S(2)}, u32[]{:S(2)}) collective-permute-start(bf16[128,512]{1,0:T(8,128)(2,1)S(1)} %collective-permute-done.9.refs_4_), channel_id=1, source_target_pairs={{0,4},{1,5},{2,6},{3,7},{4,12},{5,13},{6,14},{7,15},{8,0},{9,1},{1... | collective-permute-start | bytes 393224 | tf_op jit(solution)/shard_map/ppermute | solution.py:31
  32.8 7.1 %collective-permute-start.12 = (bf16[128,512]{1,0:T(8,128)(2,1)S(1)}, bf16[128,512]{1,0:T(8,128)(2,1)S(1)}, u32[]{:S(2)}, u32[]{:S(2)}) collective-permute-start(bf16[128,512]{1,0:T(8,128)(2,1)S(1)} %broadcast_select_fusion), channel_id=1, source_target_pairs={{0,16},{1,13},{2,18},{3,15},{4,8},{5,21},{6,10},{7,23},{8,24},{9,5... | collective-permute-start | bytes 393224 | tf_op jit(solution)/shard_map/ppermute | solution.py:31
  34.4 5.8 %collective-permute-start.10 = (bf16[128,512]{1,0:T(8,128)(2,1)S(1)}, bf16[128,512]{1,0:T(8,128)(2,1)S(1)}, u32[]{:S(2)}, u32[]{:S(2)}) collective-permute-start(bf16[128,512]{1,0:T(8,128)(2,1)S(1)} %collective-permute-done.8.refs_3_), channel_id=1, source_target_pairs={{0,8},{1,9},{2,10},{3,11},{4,0},{5,1},{6,2},{7,3},{8,16},{9,17},{1... | collective-permute-start | bytes 393224 | tf_op jit(solution)/shard_map/ppermute | solution.py:31
  41.2 1.9 %collective-permute-start.13 = (bf16[256,128]{1,0:T(8,128)(2,1)S(1)}, bf16[256,128]{1,0:T(8,128)(2,1)S(1)}, u32[]{:S(2)}, u32[]{:S(2)}) collective-permute-start(bf16[256,128]{1,0:T(8,128)(2,1)S(1)} %get-tuple-element.18), channel_id=1, source_target_pairs={{0,1},{1,0},{2,3},{3,2},{4,5},{5,4},{6,7},{7,6},{8,9},{9,8},{10,11... | collective-permute-start | bytes 196616 | tf_op jit(solution)/shard_map/ppermute | solution.py:31
  41.3 4.5 %collective-permute-start.14 = (bf16[256,128]{1,0:T(8,128)(2,1)S(1)}, bf16[256,128]{1,0:T(8,128)(2,1)S(1)}, u32[]{:S(2)}, u32[]{:S(2)}) collective-permute-start(bf16[256,128]{1,0:T(8,128)(2,1)S(1)} %get-tuple-element.19), channel_id=1, source_target_pairs={{0,2},{1,3},{2,0},{3,1},{4,6},{5,7},{6,4},{7,5},{8,10},{9,11},{10,... | collective-permute-start | bytes 196616 | tf_op jit(solution)/shard_map/ppermute | solution.py:31
  42.8 4.1 %collective-permute-start.15 = (bf16[256,128]{1,0:T(8,128)(2,1)S(1)}, bf16[256,128]{1,0:T(8,128)(2,1)S(1)}, u32[]{:S(2)}, u32[]{:S(2)}) collective-permute-start(bf16[256,128]{1,0:T(8,128)(2,1)S(1)} %get-tuple-element.20), channel_id=1, source_target_pairs={{0,3},{1,2},{2,1},{3,0},{4,7},{5,6},{6,5},{7,4},{8,11},{9,10},{10,... | collective-permute-start | bytes 196616 | tf_op jit(solution)/shard_map/ppermute | solution.py:31
